TPU v7x, 256 devices: a whole 4x4x8 slice. The times are simulated.
256 devices in a mesh: pipe: 16 (over y_hi, z), vocab: 16 (over y_lo, x, core).
Axes of the slice: x: 4, y: 4 (y_hi: 2, y_lo: 2; y = y_hi * 2 + y_lo), z: 8, core: 2. Of those that a mesh axis runs over, the one named last changes fastest.
Arguments:
- final_hidden: bfloat16 [512, 4608], P('pipe', 'vocab'), may hold values from -6 to 6
- tied_table: bfloat16 [163840, 4608], P(('pipe', 'vocab')), may hold values from -1.2 to 1.2
- target_ids: int32 [512], replicated, may hold values from 0 to 163839
- input_ids: int32 [512], replicated, may hold values from 0 to 163839
- embed_cot: bfloat16 [512, 4608], P('pipe', 'vocab'), may hold values from -0.3125 to 0.3125
Outputs:
- grad_table: bfloat16 [163840, 4608], P(('pipe', 'vocab'))
- grad_hidden: float32 [512, 4608], P('pipe', 'vocab')
- token_loss: float32 [512], P('pipe')
All inputs are finite; a program needn't handle non-finite values.
Results may differ from a plain program's by a relative error of at most 0.01.
Values may be sent and summed in bfloat16 or wider, within the bound.
A program may use at most 128 MiB of HBM per device.

v0:
```python
import jax
import jax.numpy as jnp
from jax import lax
from jax.sharding import PartitionSpec as P

D = 4608


def local(final_hidden, tied_table, target_ids, input_ids, embed_cot):
    whole_h, whole_c = (
        lax.all_gather(final_hidden, "vocab", axis=1, tiled=True),
        lax.all_gather(embed_cot, "vocab", axis=1, tiled=True),
    )
    whole_h, whole_c = (
        lax.all_gather(whole_h, "pipe", axis=0, tiled=True),
        lax.all_gather(whole_c, "pipe", axis=0, tiled=True),
    )
    rows_dev = tied_table.shape[0]
    offset = lax.axis_index(("pipe", "vocab")) * rows_dev
    vocab_ids = offset + jnp.arange(rows_dev, dtype=jnp.int32)
    logits = jnp.einsum("td,vd->tv", whole_h, tied_table, preferred_element_type=jnp.float32)
    tanh_part = jnp.tanh(logits / 30.0)
    capped = 30.0 * tanh_part
    exponent = jnp.exp(capped)
    target_mask = vocab_ids[None, :] == target_ids[:, None]
    local_sum = jnp.sum(exponent, axis=1)
    local_target = jnp.sum(jnp.where(target_mask, capped, 0.0), axis=1)
    sum_exp, target_logit = lax.psum((local_sum, local_target), ("pipe", "vocab"))
    token_loss = jnp.log(sum_exp) - target_logit
    dlogits = (
        (exponent / sum_exp[:, None] - target_mask.astype(jnp.float32))
        * (1.0 - tanh_part * tanh_part)
    ).astype(jnp.bfloat16)
    head_grad = jnp.einsum("tv,td->vd", dlogits, whole_h, preferred_element_type=jnp.float32)
    input_mask = (vocab_ids[:, None] == input_ids[None, :]).astype(jnp.bfloat16)
    embed_grad = jnp.dot(input_mask, whole_c, preferred_element_type=jnp.float32)
    grad_table = (head_grad + float(D) ** 0.5 * embed_grad).astype(jnp.bfloat16)
    products = jnp.dot(dlogits, tied_table, preferred_element_type=jnp.float32)
    partial_value = lax.psum_scatter(
        products.astype(jnp.bfloat16), "vocab", scatter_dimension=1, tiled=True
    ).astype(jnp.float32)
    grad_hidden = lax.psum_scatter(partial_value, "pipe", scatter_dimension=0, tiled=True)
    held = final_hidden.shape[0]
    loss_shard = lax.dynamic_slice_in_dim(token_loss, lax.axis_index("pipe") * held, held)
    return (grad_table, grad_hidden, loss_shard)


def solution(mesh):
    placed = (P("pipe", "vocab"), P(("pipe", "vocab"), None), P(), P(), P("pipe", "vocab"))
    return jax.shard_map(
        local,
        mesh=mesh,
        in_specs=placed,
        out_specs=(P(("pipe", "vocab"), None), P("pipe", "vocab"), P("pipe")),
        check_vma=False,
    )
```

profile of v0, /device:TPU:1, one launch (start us, length us, event | category | flops | bytes accessed | tf_op | source)
XLA Modules:
  0.0 604.8 jit_solution(8618035419654364876)
XLA Ops:
  7.2 0.0 copy-start
  7.2 0.0 all-gather.5.cloned.1.call-start
  7.2 22.3 %all-gather = bf16[16,288,32]{1,2,0:T(8,128)(2,1)S(1)} all-gather(bf16[1,288,32]{1,2,0:T(8,128)(2,1)} %bitcast.20), channel_id=1, replica_groups=mesh['pipe'=16,'vocab'=16] {'vocab'}, dimensions={0}, use_global_device_ids=true | all-gather | bytes 313344 | tf_op jit(solution)/shard_map/all_gather | solution.py:11
  29.6 0.1 copy.12
  29.7 1.1 reshape.18
  30.8 0.0 all-gather.5.cloned.1.call-update
  30.8 0.0 reduce-scatter.5.cloned.1.call-start
  30.9 100.0 %all-gather.5.cloned.1.call-done = bf16[512,4608]{1,0:T(8,128)(2,1)} async-done(((bf16[32,4608]{1,0:T(8,128)(2,1)}), bf16[512,4608]{1,0:T(8,128)(2,1)}) %all-gather.5.cloned.1.call-update) | async-done | bytes 4718608 | tf_op jit(solution)/shard_map/all_gather | solution.py:15
  130.9 0.0 copy-done
  130.9 7.8 %fusion.4 = (f32[512]{0:T(512)S(1)}, f32[512]{0:T(512)S(1)}, f32[512,640]{1,0:T(8,128)S(1)}) fusion(s32[640]{0:T(1024)S(1)} %iota_add_fusion, s32[512]{0:T(512)S(1)} %copy-done, bf16[512,4608]{1,0:T(8,128)(2,1)} %all-gather.5.cloned.1.call-done, bf16[640,4608]{1,0:T(8,128)(2,1)} %param.6), kind=kOutput, calls=%fused_computation.9 | convolution fusion | flops 3021863936 | bytes 11936256 | tf_op jit(solution)/shard_map/td,vd->tv/dot_general | solution.py:21
  138.7 77.8 %all-reduce = (f32[512]{0:T(512)S(1)}, f32[512]{0:T(512)S(1)}) all-reduce(f32[512]{0:T(512)S(1)} %get-tuple-element.13, f32[512]{0:T(512)S(1)} %get-tuple-element.12), channel_id=1, replica_groups=mesh['pipe'=16,'vocab'=16] {'pipe','vocab'}, use_global_device_ids=true, to_apply=%region_1.2 | all-reduce | flops 1024 | bytes 8192 | tf_op jit(solution)/shard_map/psum | solution.py:28
  216.5 9.8 %convolution_convert_fusion = bf16[512,4608]{0,1:T(8,128)(2,1)} fusion(bf16[640,4608]{1,0:T(8,128)(2,1)} %param.6, f32[512,640]{1,0:T(8,128)S(1)} %get-tuple-element.16, s32[640]{0:T(1024)S(1)} %iota_add_fusion, f32[512]{0:T(512)S(1)} %get-tuple-element.14, s32[512]{0:T(512)S(1)} %copy-done), kind=kOutput, calls=%fused_computation.1 | convolution fusion | flops 3025207296 | bytes 11934208 | tf_op jit(solution)/shard_map/dot_general | solution.py:38
  226.3 0.0 copy-start.1
  226.3 0.0 reduce-scatter.5.cloned.1.call-update
  226.3 0.0 all-gather.7.cloned.1.call-start
  226.4 0.7 copy-done.1
  227.0 19.6 %all-gather.1 = bf16[16,288,32]{1,2,0:T(8,128)(2,1)S(1)} all-gather(bf16[1,288,32]{1,2,0:T(8,128)(2,1)S(1)} %bitcast.21), channel_id=1, replica_groups=mesh['pipe'=16,'vocab'=16] {'vocab'}, dimensions={0}, use_global_device_ids=true | all-gather | bytes 313344 | tf_op jit(solution)/shard_map/all_gather | solution.py:12
  246.6 0.1 copy.13
  246.8 1.1 reshape.20
  247.9 0.0 all-gather.7.cloned.1.call-update
  247.9 0.2 reduce-scatter.7.cloned.1.call-start
  248.1 10.2 %fusion.9 = f32[640,4608]{1,0:T(8,128)} fusion(bf16[512,4608]{1,0:T(8,128)(2,1)} %all-gather.5.cloned.1.call-done, f32[512,640]{1,0:T(8,128)S(1)} %get-tuple-element.16, s32[640]{0:T(1024)S(1)} %iota_add_fusion, f32[512]{0:T(512)S(1)} %get-tuple-element.14, s32[512]{0:T(512)S(1)} %copy-done), kind=kOutput, calls=%fused_computation.16 | convolution fusion | flops 3022848000 | bytes 17832448 | tf_op jit(solution)/shard_map/tv,td->vd/dot_general | solution.py:34
  258.4 0.0 copy-start.2
  258.4 31.1 %reduce-scatter.5.cloned.1.call-done = bf16[512,288]{0,1:T(8,128)(2,1)} async-done(((bf16[512,4608]{0,1:T(8,128)(2,1)}), bf16[512,288]{0,1:T(8,128)(2,1)}) %reduce-scatter.5.cloned.1.call-update) | async-done | bytes 294928 | tf_op jit(solution)/shard_map/reduce_scatter | solution.py:39
  289.4 2.0 copy.15
  291.5 0.0 reduce-scatter.7.cloned.1.call-update
  291.5 0.6 dynamic_slice.3
  292.1 102.6 %all-gather.7.cloned.1.call-done = bf16[512,4608]{1,0:T(8,128)(2,1)} async-done(((bf16[32,4608]{1,0:T(8,128)(2,1)}), bf16[512,4608]{1,0:T(8,128)(2,1)}) %all-gather.7.cloned.1.call-update) | async-done | bytes 4718608 | tf_op jit(solution)/shard_map/all_gather | solution.py:16
  394.7 0.0 copy-done.2
  394.7 9.3 %add_convert_fusion = bf16[640,4608]{1,0:T(8,128)(2,1)} fusion(f32[640,4608]{1,0:T(8,128)} %fusion.9, bf16[512,4608]{1,0:T(8,128)(2,1)} %all-gather.7.cloned.1.call-done, s32[512]{0:T(512)S(1)} %copy-done.2, s32[640]{0:T(1024)S(1)} %iota_add_fusion), kind=kOutput, calls=%fused_computation | convolution fusion | flops 3029073920 | bytes 22417920 | tf_op jit(solution)/shard_map/dot_general | solution.py:36
  404.0 194.3 %reduce-scatter.7.cloned.1.call-done = f32[32,288]{1,0:T(8,128)} async-done(((f32[512,288]{1,0:T(8,128)}), f32[32,288]{1,0:T(8,128)}) %reduce-scatter.7.cloned.1.call-update) | async-done | bytes 36880
  (2 shorter events, 0.0 us)
Async XLA Ops:
  7.2 123.8 %copy-start = (s32[512]{0:T(512)S(1)}, s32[512]{0:T(512)}, u32[]{:S(2)}) copy-start(s32[512]{0:T(512)} %param.7) | copy-start | bytes 6148
  7.2 123.7 %all-gather.5.cloned.1.call-start = ((), (), s32[]{:S(2)}) async-start(), calls=%async_computation.2 | async-start | bytes 5013504 | tf_op jit(solution)/shard_map/all_gather | solution.py:15
  30.8 258.6 %reduce-scatter.5.cloned.1.call-start = ((), (), s32[]{:S(2)}) async-start(), calls=%async_computation.4 | async-start | bytes 5013504 | tf_op jit(solution)/shard_map/reduce_scatter | solution.py:39
  226.3 0.7 copy-start.1
  226.3 168.4 %all-gather.7.cloned.1.call-start = ((), (), s32[]{:S(2)}) async-start(), calls=%async_computation.3 | async-start | bytes 5013504 | tf_op jit(solution)/shard_map/all_gather | solution.py:16
  247.9 350.3 %reduce-scatter.7.cloned.1.call-start = ((), (), s32[]{:S(2)}) async-start(), calls=%async_computation.5 | async-start | bytes 835584
  258.4 136.4 %copy-start.2 = (s32[512]{0:T(512)S(1)}, s32[512]{0:T(512)}, u32[]{:S(2)}) copy-start(s32[512]{0:T(512)} %param.8) | copy-start | bytes 6148
Sparse Core Ops, SparseCore 0:
  30.9 99.9 all-gather.4
  226.4 62.9 reduce-scatter.4
  292.0 102.6 all-gather.6
  399.0 199.2 reduce-scatter.6
where the time goes:
time: 610 us; the launch traced here: 605 us
  waiting for transfers between devices  428 us (70%)
  blocking collectives  120 us (20%)
  matrix products  37 us (6%)
  between operations  13.8 us (2%)
    unnamed x5, waiting for transfers between devices  194 us
    all_gather x1, waiting for transfers between devices, local(): lax.all_gather(whole_c, 'pipe', axis=0, tiled=True)  103 us
    all_gather x1, waiting for transfers between devices, local(): lax.all_gather(whole_h, 'pipe', axis=0, tiled=True)  100 us
    psum x1, blocking collectives, local(): lax.psum((local_sum, local_target), ('pipe', 'vocab'))  77.8 us
    reduce_scatter x1, waiting for transfers between devices, local(): lax.psum_scatter(products.astype(jnp.bfloat16), 'vocab', scatter_dimensio...  31.1 us
    all_gather x1, blocking collectives, local(): lax.all_gather(final_hidden, 'vocab', axis=1, tiled=True)  22.3 us
    all_gather x1, blocking collectives, local(): lax.all_gather(embed_cot, 'vocab', axis=1, tiled=True)  19.6 us
  transfers between devices with their start and end apart: 4, of which 4 were waited for; matrix products, arithmetic and copies ran while one was open for 4% of the time, Pallas kernels for 0%

commit v1 on v0

v1 whole, which is shorter than its diff:
```python
import jax
import jax.numpy as jnp
from jax import lax
from jax.experimental import pallas as pl
from jax.experimental.pallas import tpu as pltpu
from jax.sharding import PartitionSpec as P

D = 4608
HALF = D // 2
ROWS = 640
TOKENS = 512
PIECE = 288
BF = jnp.bfloat16
F32 = jnp.float32
MESH = pl.DeviceIdType.MESH
NT = (((1,), (1,)), ((), ()))


def rcopy(src, dst, send, recv, p, v):
    return pltpu.make_async_remote_copy(
        src_ref=src, dst_ref=dst, send_sem=send, recv_sem=recv, device_id=(p, v), device_id_type=MESH
    )


def kernel(
    h_in, w_hbm, tgt_ref, ids_ref, c_in,
    grad_out, hid_out, loss_out,
    w, h_buf, c_buf, tanh_buf, dl, dlt, pair, rbuf, g_buf,
    s1, ar_src, ar_v, ar_p, y_buf, v_src, v_buf,
    w_sem, s1s, s1r, ys, yr, zs, zr, cs, cr, avs, avr, aps, apr, ps, pr, rs, rr, yys, yyr, vs, vr,
):
    p = lax.axis_index("pipe")
    v = lax.axis_index("vocab")
    zz = lax.rem(p, 8)
    yh = p // 8
    core = lax.rem(v, 2)
    mate = v + 1 - 2 * core
    other_y = lax.rem(p + 8, 16)
    zup = yh * 8 + lax.rem(zz + 1, 8)
    zdn = yh * 8 + lax.rem(zz + 7, 8)
    wcopy = pltpu.make_async_copy(w_hbm, w, w_sem)
    wcopy.start()

    bar = pltpu.get_barrier_semaphore()

    @pl.loop(1, 16)
    def _(i):
        pl.semaphore_signal(bar, inc=1, device_id=(p, lax.rem(v + i, 16)), device_id_type=MESH)
        pl.semaphore_signal(bar, inc=1, device_id=(lax.rem(p + i, 16), v), device_id_type=MESH)

    pl.semaphore_wait(bar, 30)

    bufs = (h_buf, c_buf)
    ins = (h_in, c_in)

    def s1copy(a, i):
        return rcopy(ins[a], s1.at[a, v], s1s.at[a, i], s1r.at[a, i], p, lax.rem(v + i, 16))

    for a in range(2):
        @pl.loop(1, 16)
        def _(i):
            s1copy(a, i).start()
    cols = pl.ds(pl.multiple_of(core * HALF, 128), HALF)
    mate_cols = pl.ds(pl.multiple_of((1 - core) * HALF, 128), HALF)
    s1[0, pl.ds(v, 1)] = h_in[...][None]
    s1[1, pl.ds(v, 1)] = c_in[...][None]

    def s1_finish(a):
        @pl.loop(1, 16)
        def _(i):
            s1copy(a, i).wait_recv()
        bufs[a][yh, zz] = jnp.concatenate([s1[a, k] for k in range(16)], axis=-1)

    def blk(a, y, z):
        return bufs[a].at[y, z, :, cols]

    def ycopy(a):
        return rcopy(blk(a, yh, zz), blk(a, yh, zz), ys.at[a], yr.at[a], other_y, v)

    def zcopy(a, d, s, k):
        y = yh if k == 0 else 1 - yh
        z = lax.rem(zz - s + 8, 8) if d == 0 else lax.rem(zz + s, 8)
        return rcopy(blk(a, y, z), blk(a, y, z), zs.at[a, d, s, k], zr.at[a, d, s, k], zup if d == 0 else zdn, v)

    def mcopy(a, y, z):
        return rcopy(blk(a, y, z), blk(a, y, z), cs.at[a, y, z], cr.at[a, y, z], p, mate)

    def has(d, s, k):
        return s < 3 or k == d

    def arrived(d, s, k):
        y = yh if k == 0 else 1 - yh
        z = lax.rem(zz - s - 1 + 8, 8) if d == 0 else lax.rem(zz + s + 1, 8)
        return y, z

    def ring_begin(a):
        ycopy(a).start()
        for d in range(2):
            zcopy(a, d, 0, 0).start()

    def ring_second(a):
        ycopy(a).wait_recv()
        for d in range(2):
            zcopy(a, d, 0, 1).start()
        mcopy(a, 1 - yh, zz).start()

    def ring_step(a, s):
        for k in range(2):
            for d in range(2):
                if has(d, s, k):
                    zcopy(a, d, s, k).wait_recv()
                    if s < 3 and has(d, s + 1, k):
                        zcopy(a, d, s + 1, k).start()
                    mcopy(a, *arrived(d, s, k)).start()

    def ring_finish(a):
        mcopy(a, 1 - yh, zz).wait_recv()
        for s in range(4):
            for k in range(2):
                for d in range(2):
                    if has(d, s, k):
                        mcopy(a, *arrived(d, s, k)).wait_recv()

    def ring_drain(a):
        ycopy(a).wait_send()
        mcopy(a, 1 - yh, zz).wait_send()
        for s in range(4):
            for k in range(2):
                for d in range(2):
                    if has(d, s, k):
                        mcopy(a, *arrived(d, s, k)).wait_send()
                        zcopy(a, d, s, k).wait_send()

        @pl.loop(1, 16)
        def _(i):
            s1copy(a, i).wait_send()

    s1_finish(0)
    ring_begin(0)
    ring_second(0)
    s1_finish(1)
    for s in range(4):
        ring_step(0, s)
    ring_begin(1)
    ring_finish(0)
    ring_second(1)
    wcopy.wait()

    base = (p * 16 + v) * ROWS
    tgt = tgt_ref[...]

    def row_ids(i, rows):
        return base + i * rows + lax.broadcasted_iota(jnp.int32, (rows, TOKENS), 0)

    ar_src[...] = jnp.zeros_like(ar_src)

    @pl.loop(0, 5)
    def _(i):
        r = pl.ds(pl.multiple_of(i * 128, 128), 128)
        logits = lax.dot_general(w[r, :], h_buf[...].reshape(TOKENS, D), NT, preferred_element_type=F32)
        t = jnp.tanh(logits / 30.0)
        tanh_buf[r, :] = t
        capped = 30.0 * t
        ar_src[0:1, :] += jnp.sum(jnp.exp(capped), axis=0, keepdims=True)
        ar_src[1:2, :] += jnp.sum(jnp.where(row_ids(i, 128) == tgt, capped, 0.0), axis=0, keepdims=True)

    def avcopy(i):
        return rcopy(ar_src, ar_v.at[v], avs.at[i], avr.at[i], p, lax.rem(v + i, 16))

    def apcopy(i):
        return rcopy(ar_src, ar_p.at[p], aps.at[i], apr.at[i], lax.rem(p + i, 16), v)

    @pl.loop(1, 16)
    def _(i):
        avcopy(i).start()
    ar_v[pl.ds(v, 1)] = ar_src[...][None]

    @pl.loop(1, 16)
    def _(i):
        avcopy(i).wait()
    ar_src[...] = jnp.sum(ar_v[...], axis=0)

    @pl.loop(1, 16)
    def _(i):
        apcopy(i).start()
    ar_p[pl.ds(p, 1)] = ar_src[...][None]

    @pl.loop(1, 16)
    def _(i):
        apcopy(i).wait()
    sums = jnp.sum(ar_p[...], axis=0)
    sum_exp = sums[0:1, :]
    loss_out[...] = jnp.log(sum_exp) - sums[1:2, :]

    @pl.loop(0, 5)
    def _(i):
        r = pl.ds(pl.multiple_of(i * 128, 128), 128)
        t = tanh_buf[r, :]
        hit = (row_ids(i, 128) == tgt).astype(F32)
        d = (jnp.exp(30.0 * t) / sum_exp - hit) * (1.0 - t * t)
        dlt[r, :] = d.astype(BF)
        dl[:, r] = d.T.astype(BF)

    ring_step(1, 0)

    @pl.loop(0, 9)
    def _(i):
        n = pl.ds(pl.multiple_of(i * 512, 512), 512)
        g = jnp.dot(dl[...], w[:, n], preferred_element_type=F32)
        g_buf[:, :, :, n] = g.astype(BF).reshape(2, 8, 32, 512)

    ring_step(1, 1)
    ring_step(1, 2)
    ring_step(1, 3)

    def pcopy(j):
        z = lax.rem(zz + j, 8)
        return rcopy(g_buf.at[:, z, :, mate_cols], pair.at[:, z], ps.at[j], pr.at[j], p, mate)

    order = (4, 3, 5, 2, 6, 1, 7, 0)
    for j in order:
        pcopy(j).start()

    def rdest(d, s):
        return lax.rem(zz + 4 - s, 8) if d == 0 else lax.rem(zz + 4 + s, 8)

    def rsend(d, s, y):
        z = rdest(d, s)
        return rcopy(pair.at[y, z], rbuf.at[d, s, y], rs.at[d, s, y], rr.at[d, s, y], zup if d == 0 else zdn, v)

    def rhas(d, s, y):
        return s > 0 or y == d

    def own(y, z):
        return g_buf[y, z, :, cols].astype(F32) + pair[y, z].astype(F32)

    for s in range(4):
        for d in range(2):
            if s == 0:
                if d == 0:
                    pcopy(4).wait_recv()
            else:
                pcopy(4 - s if d == 0 else 4 + s).wait_recv()
            for y in range(2):
                if rhas(d, s, y):
                    total = own(y, rdest(d, s))
                    if s > 0 and rhas(d, s - 1, y):
                        rsend(d, s - 1, y).wait_recv()
                        total += rbuf[d, s - 1, y].astype(F32)
                    pair[y, rdest(d, s)] = total.astype(BF)
                    rsend(d, s, y).start()

    ring_finish(1)

    @pl.loop(0, 9)
    def _(i):
        n = pl.ds(pl.multiple_of(i * 512, 512), 512)
        sel = (
            base + lax.broadcasted_iota(jnp.int32, (ROWS, TOKENS), 0) == ids_ref[...]
        ).astype(F32).astype(BF)
        acc = jnp.dot(sel, c_buf[:, :, :, n].reshape(TOKENS, 512), preferred_element_type=F32) * (float(D) ** 0.5)
        acc += jnp.dot(dlt[...], h_buf[:, :, :, n].reshape(TOKENS, 512), preferred_element_type=F32)
        grad_out[:, n] = acc.astype(BF)

    pcopy(0).wait_recv()

    def final(y):
        total = own(y, zz)
        for d in range(2):
            total += rbuf[d, 3, y].astype(F32)
        return total

    for d in range(2):
        for y in range(2):
            rsend(d, 3, y).wait_recv()
    ycp = rcopy(y_buf.at[0], y_buf.at[1], yys, yyr, other_y, v)
    y_buf[0] = final(1 - yh).astype(BF)
    ycp.start()
    mine = final(yh)
    ycp.wait()
    mine += y_buf[1].astype(F32)

    def vcopy(k):
        return rcopy(v_src.at[k], v_buf.at[v // 2], vs.at[k], vr.at[v // 2], p, core * 8 + k)

    for k in range(8):
        v_src[k] = mine[:, k * PIECE : (k + 1) * PIECE]
    for k in range(8):
        @pl.when(core * 8 + k != v)
        def _():
            vcopy(k).start()

        @pl.when(core * 8 + k == v)
        def _():
            v_buf[pl.ds(v // 2, 1)] = v_src[k][None]
    for j in range(8):
        @pl.when(2 * j + v // 8 != v)
        def _():
            rcopy(v_src.at[0], v_buf.at[j], vs.at[0], vr.at[j], p, mate).wait_recv()
    hid_out[...] = jnp.sum(v_buf[...], axis=0)

    for k in range(8):
        @pl.when(core * 8 + k != v)
        def _():
            vcopy(k).wait_send()
    for a in range(2):
        ring_drain(a)
    for j in order:
        pcopy(j).wait_send()
    for s in range(4):
        for d in range(2):
            for y in range(2):
                if rhas(d, s, y):
                    rsend(d, s, y).wait_send()


def local(final_hidden, tied_table, target_ids, input_ids, embed_cot):
    vm = pl.BlockSpec(memory_space=pltpu.VMEM)
    sem = pltpu.SemaphoreType.DMA
    grad, hid, loss = pl.pallas_call(
        kernel,
        out_shape=[
            jax.ShapeDtypeStruct((ROWS, D), BF),
            jax.ShapeDtypeStruct((32, PIECE), F32),
            jax.ShapeDtypeStruct((1, TOKENS), F32),
        ],
        in_specs=[vm, pl.BlockSpec(memory_space=pl.ANY), vm, vm, vm],
        out_specs=[vm, vm, vm],
        scratch_shapes=[
            pltpu.VMEM((ROWS, D), BF),
            pltpu.VMEM((2, 8, 32, D), BF),
            pltpu.VMEM((2, 8, 32, D), BF),
            pltpu.VMEM((ROWS, TOKENS), F32),
            pltpu.VMEM((TOKENS, ROWS), BF),
            pltpu.VMEM((ROWS, TOKENS), BF),
            pltpu.VMEM((2, 8, 32, HALF), BF),
            pltpu.VMEM((2, 4, 2, 32, HALF), BF),
            pltpu.VMEM((2, 8, 32, D), BF),
            pltpu.VMEM((2, 16, 32, PIECE), BF),
            pltpu.VMEM((8, TOKENS), F32),
            pltpu.VMEM((16, 8, TOKENS), F32),
            pltpu.VMEM((16, 8, TOKENS), F32),
            pltpu.VMEM((2, 32, HALF), BF),
            pltpu.VMEM((8, 32, PIECE), F32),
            pltpu.VMEM((8, 32, PIECE), F32),
            sem, sem((2, 16)), sem((2, 16)), sem((2,)), sem((2,)),
            sem((2, 2, 4, 2)), sem((2, 2, 4, 2)), sem((2, 2, 8)), sem((2, 2, 8)),
            sem((16,)), sem((16,)), sem((16,)), sem((16,)),
            sem((8,)), sem((8,)), sem((2, 4, 2)), sem((2, 4, 2)), sem, sem, sem((8,)), sem((8,)),
        ],
        compiler_params=pltpu.CompilerParams(
            collective_id=0, has_side_effects=True, vmem_limit_bytes=63 << 20
        ),
        name="head_backward",
    )(
        final_hidden,
        tied_table,
        target_ids.reshape(1, TOKENS),
        input_ids.reshape(1, TOKENS),
        embed_cot,
    )
    held = final_hidden.shape[0]
    loss_shard = lax.dynamic_slice_in_dim(loss[0], lax.axis_index("pipe") * held, held)
    return (grad, hid, loss_shard)


def solution(mesh):
    placed = (P("pipe", "vocab"), P(("pipe", "vocab"), None), P(), P(), P("pipe", "vocab"))
    return jax.shard_map(
        local,
        mesh=mesh,
        in_specs=placed,
        out_specs=(P(("pipe", "vocab"), None), P("pipe", "vocab"), P("pipe")),
        check_vma=False,
    )
```

time: 610 us -> 155 us (0.25)
  waiting for transfers between devices: 428 us -> 0 us
  Pallas kernels: 0 us -> 147 us
  blocking collectives: 120 us -> 0 us
  matrix products: 37 us -> 0 us
  between operations: 13.8 us -> 0.65 us
    all_gather x2 -> x0, waiting for transfers between devices: 203 us -> none  [the longest x1 103 us: local(): lax.all_gather(whole_c, 'pipe', axis=0, tiled=True)]
    unnamed x5 -> x0, waiting for transfers between devices: 194 us -> none
    pallas_call x0 -> x1, Pallas kernels: none -> 147 us  [local(): pl.pallas_call(kernel, out_shape=[jax.ShapeDtypeStruct((ROWS, D), BF), ja...]
    psum x1 -> x0, blocking collectives: 77.8 us -> none  [local(): lax.psum((local_sum, local_target), ('pipe', 'vocab'))]
    all_gather x2 -> x0, blocking collectives: 41.9 us -> none  [the longest x1 22.3 us: local(): lax.all_gather(final_hidden, 'vocab', axis=1, tiled=True)]
    dot_general x4 -> x0, matrix products: 37 us -> none  [the longest x1 10.2 us: local(): jnp.einsum('tv,td->vd', dlogits, whole_h, preferred_element_type=jnp.floa...]
    reduce_scatter x1 -> x0, waiting for transfers between devices: 31.1 us -> none  [local(): lax.psum_scatter(products.astype(jnp.bfloat16), 'vocab', scatter_dimensio...]
  transfers between devices with their start and end apart: 4 -> 0, of which waited for: 4 -> 0; matrix products, arithmetic and copies ran while one was open for 4% -> 0% of each run, Pallas kernels for 0% -> 0%
where the time goes in v1:
time: 155 us
  Pallas kernels  147 us (95%)
  local copies, waits for them, and re-layouts  7.45 us (5%)
    pallas_call x1, Pallas kernels, local(): pl.pallas_call(kernel, out_shape=[jax.ShapeDtypeStruct((ROWS, D), BF), ja...  147 us
    unnamed x4, local copies, waits for them, and re-layouts  6.25 us

profile of v1, /device:TPU:1, one launch (start us, length us, event | category | flops | bytes accessed | tf_op | source)
XLA Modules:
  0.0 155.1 jit_solution(4030900856537282665)
XLA Ops:
  0.6 147.0 %head_backward.1 = (bf16[640,4608]{1,0:T(8,128)(2,1)}, f32[32,288]{1,0:T(8,128)}, f32[1,512]{1,0:T(1,128)}) custom-call(bf16[32,288]{1,0:T(8,128)(2,1)} %h_in.1, bf16[640,4608]{1,0:T(8,128)(2,1)} %w_hbm.1, s32[1,512]{1,0:T(1,128)} %bitcast.4, s32[1,512]{1,0:T(1,128)} %bitcast.5, bf16[32,288]{1,0:T(8,128)(2,1)} %c_in.1), custom_call_target="tpu_custom_call" | custom-call | tf_op jit(solution)/shard_map/head_backward/pallas_call | solution.py:320
  147.7 1.2 dynamic-slice_bitcast_fusion
  148.9 0.0 copy-start
  148.9 5.6 %copy.10 = bf16[640,4608]{1,0:T(8,128)(2,1)} copy(bf16[640,4608]{1,0:T(8,128)(2,1)} %get-tuple-element.12) | data formatting | bytes 11796480
  154.5 0.0 copy-done
  154.5 0.6 copy.11
Async XLA Ops:
  148.9 5.6 %copy-start = (f32[32,288]{1,0:T(8,128)S(1)}, f32[32,288]{1,0:T(8,128)}, u32[]{:S(2)}) copy-start(f32[32,288]{1,0:T(8,128)} %get-tuple-element.13) | copy-start | bytes 110596

commit v2 on v1

v2 whole, which is shorter than its diff:
```python
import jax
import jax.numpy as jnp
from jax import lax
from jax.experimental import pallas as pl
from jax.experimental.pallas import tpu as pltpu
from jax.sharding import PartitionSpec as P

D = 4608
HALF = D // 2
QUART = D // 4
LAG = 5
RLAG = 3
SLOTS = 15 + 2 * LAG
ROWS = 640
TOKENS = 512
PIECE = 288
BF = jnp.bfloat16
F32 = jnp.float32
MESH = pl.DeviceIdType.MESH
NT = (((1,), (1,)), ((), ()))


def rcopy(src, dst, send, recv, p, v):
    return pltpu.make_async_remote_copy(
        src_ref=src, dst_ref=dst, send_sem=send, recv_sem=recv, device_id=(p, v), device_id_type=MESH
    )


def kernel(
    h_in, w_hbm, tgt_ref, ids_ref, c_in,
    grad_out, hid_out, loss_out,
    w, h_buf, c_buf, tanh_buf, dl, dlt, pair, rbuf, g_buf,
    s1, ar_src, ar_v, ar_p, y_buf, v_src, v_buf,
    xr1, xr2,
    w_sem, s1s, s1r, ys, yr, zs, zr, cs, cr, avs, avr, aps, apr, ps, pr, rs, rr, yys, yyr, vs, vr,
    xs, xr, x1s, x1r, x2s, x2r, gs, g_stage,
):
    p = lax.axis_index("pipe")
    v = lax.axis_index("vocab")
    zz = lax.rem(p, 8)
    yh = p // 8
    core = lax.rem(v, 2)
    mate = v + 1 - 2 * core
    xx = lax.rem(v // 2, 4)
    ylo = v // 8
    x_at = lambda i: lax.rem(xx + i, 4)
    x_dev = lambda i: ylo * 8 + x_at(i) * 2 + core
    other_y = lax.rem(p + 8, 16)
    zup = yh * 8 + lax.rem(zz + 1, 8)
    zdn = yh * 8 + lax.rem(zz + 7, 8)
    wcopy = pltpu.make_async_copy(w_hbm, w, w_sem)
    wcopy.start()

    bar = pltpu.get_barrier_semaphore()

    @pl.loop(1, 16)
    def _(i):
        pl.semaphore_signal(bar, inc=1, device_id=(p, lax.rem(v + i, 16)), device_id_type=MESH)
        pl.semaphore_signal(bar, inc=1, device_id=(lax.rem(p + i, 16), v), device_id_type=MESH)

    pl.semaphore_wait(bar, 30)

    bufs = (h_buf, c_buf)
    ins = (h_in, c_in)

    def s1dev(i):
        return lax.rem(v // 2 + i, 8) * 2 + ylo

    def s1copy(a, i):
        return rcopy(ins[a], s1.at[a, lax.rem(v, 8)], s1s.at[a, i], s1r.at[a, lax.rem(v, 8)], p, s1dev(i))

    def s1_begin(a):
        @pl.loop(1, 8)
        def _(i):
            s1copy(a, i).start()

        @pl.when(core != ylo)
        def _():
            s1copy(a, 0).start()

        @pl.when(core == ylo)
        def _():
            s1[a, pl.ds(lax.rem(v, 8), 1)] = ins[a][...][None]

    mate_cols = pl.ds(pl.multiple_of((1 - core) * HALF, 128), HALF)

    def s1_finish(a):
        @pl.loop(0, 8)
        def _(j):
            @pl.when(core * 8 + j != v)
            def _():
                rcopy(ins[a], s1.at[a, j], s1s.at[a, 0], s1r.at[a, j], p, mate).wait_recv()

        block = jnp.concatenate([s1[a, k] for k in range(8)], axis=-1)
        for c in range(2):
            @pl.when(core == c)
            def _():
                bufs[a][yh, zz, :, c * HALF : (c + 1) * HALF] = block

    def s1_drain(a):
        @pl.loop(1, 8)
        def _(i):
            s1copy(a, i).wait_send()

        @pl.when(core != ylo)
        def _():
            s1copy(a, 0).wait_send()

    s1_begin(0)

    def piece(ref, y, z, x):
        return ref.at[
            y, z, pl.ds(pl.multiple_of(lax.rem(x, 2) * 16, 16), 16), pl.ds(pl.multiple_of(x // 2 * QUART, 128), QUART)
        ]

    def part(ref, c, y, z):
        return piece(ref, y, z, xx) if c == 0 else ref.at[y, z, :, pl.ds(HALF, HALF)]

    def ycopy(c, a):
        b = part(bufs[a], c, yh, zz)
        return rcopy(b, b, ys.at[a], yr.at[a], other_y, v)

    def zcopy(c, a, d, s, k):
        y = yh if k == 0 else 1 - yh
        z = lax.rem(zz - s + 8, 8) if d == 0 else lax.rem(zz + s, 8)
        b = part(bufs[a], c, y, z)
        return rcopy(b, b, zs.at[a, d, s, k], zr.at[a, d, s, k], zup if d == 0 else zdn, v)

    def mcopy(c, a, y, z):
        b = bufs[a].at[y, z, :, pl.ds(c * HALF, HALF)]
        return rcopy(b, b, cs.at[a, y, z], cr.at[a, y, z], p, mate)

    def xcopy(a, d, hop, y, z):
        b = piece(bufs[a], y, z, xx if hop == 0 else x_at(3 if d == 0 else 1))
        return rcopy(b, b, xs.at[a, d, hop, y, z], xr.at[a, d, hop, y, z], p, x_dev(1 if d == 0 else 3))

    def has(d, s, k):
        return s < 3 or k == d

    events = [None] + [(s, k, d) for s in range(4) for k in range(2) for d in range(2) if has(d, s, k)]

    def where(e):
        if e is None:
            return 1, 1 - yh, zz
        s, k, d = e
        z = lax.rem(zz - s - 1 + 8, 8) if d == 0 else lax.rem(zz + s + 1, 8)
        return k, (yh if k == 0 else 1 - yh), z

    def on_core(c):
        return pl.when(core == c)

    def ring_begin(a):
        for c in range(2):
            @on_core(c)
            def _():
                ycopy(c, a).start()
                for d in range(2):
                    zcopy(c, a, d, 0, 0).start()
                mcopy(c, a, yh, zz).start()

    def take(c, a, e):
        k, y, z = where(e)
        if e is None:
            ycopy(c, a).wait_recv()
            for d in range(2):
                zcopy(c, a, d, 0, 1).start()
        else:
            s, k, d = e
            zcopy(c, a, d, s, k).wait_recv()
            if s < 3 and has(d, s + 1, k):
                zcopy(c, a, d, s + 1, k).start()
        if c == 1:
            mcopy(c, a, y, z).start()
        else:
            for d in range(2):
                xcopy(a, d, 0, y, z).start()

    def ring_slots(a, lo, hi):
        @on_core(0)
        def _():
            for i in range(lo, hi):
                if i < 15:
                    take(0, a, events[i])
                if LAG <= i < 15 + LAG:
                    k, y, z = where(events[i - LAG])
                    for d in range(2):
                        xcopy(a, d, 0, y, z).wait_recv()
                    xcopy(a, k, 1, y, z).start()
                if i >= 2 * LAG:
                    k, y, z = where(events[i - 2 * LAG])
                    xcopy(a, k, 1, y, z).wait_recv()
                    mcopy(0, a, y, z).start()

        @on_core(1)
        def _():
            for i in range(min(lo, 15), min(hi, 15)):
                take(1, a, events[i])

    def ring_finish(a):
        for c in range(2):
            @on_core(c)
            def _():
                mcopy(1 - c, a, yh, zz).wait_recv()
                for e in events:
                    _, y, z = where(e)
                    mcopy(1 - c, a, y, z).wait_recv()

    def ring_drain(a):
        for c in range(2):
            @on_core(c)
            def _():
                ycopy(c, a).wait_send()
                mcopy(c, a, yh, zz).wait_send()
                for e in events:
                    k, y, z = where(e)
                    mcopy(c, a, y, z).wait_send()
                    if c == 0:
                        for d in range(2):
                            xcopy(a, d, 0, y, z).wait_send()
                        xcopy(a, k, 1, y, z).wait_send()
                    if e is not None:
                        s, k, d = e
                        zcopy(c, a, d, s, k).wait_send()

        s1_drain(a)

    s1_finish(0)
    ring_begin(0)
    s1_begin(1)
    ring_slots(0, 0, 9)
    s1_finish(1)
    ring_slots(0, 9, SLOTS)
    ring_begin(1)
    ring_finish(0)
    wcopy.wait()

    base = (p * 16 + v) * ROWS
    tgt = tgt_ref[...]

    def row_ids(i, rows):
        return base + i * rows + lax.broadcasted_iota(jnp.int32, (rows, TOKENS), 0)

    ar_src[...] = jnp.zeros_like(ar_src)

    for i in range(5):
        r = slice(i * 128, (i + 1) * 128)
        logits = lax.dot_general(w[r, :], h_buf[...].reshape(TOKENS, D), NT, preferred_element_type=F32)
        t = jnp.tanh(logits / 30.0)
        tanh_buf[r, :] = t
        capped = 30.0 * t
        ar_src[0:1, :] += jnp.sum(jnp.exp(capped), axis=0, keepdims=True)
        ar_src[1:2, :] += jnp.sum(jnp.where(row_ids(i, 128) == tgt, capped, 0.0), axis=0, keepdims=True)
        ring_slots(1, 2 * i, 2 * i + 2)

    def avcopy(i):
        return rcopy(ar_src, ar_v.at[v], avs.at[i], avr.at[i], p, lax.rem(v + i, 16))

    def apcopy(i):
        return rcopy(ar_src, ar_p.at[p], aps.at[i], apr.at[i], lax.rem(p + i, 16), v)

    @pl.loop(1, 16)
    def _(i):
        avcopy(i).start()
    ar_v[pl.ds(v, 1)] = ar_src[...][None]
    ring_slots(1, 10, 14)

    @pl.loop(1, 16)
    def _(i):
        avcopy(i).wait()
    ar_src[...] = jnp.sum(ar_v[...], axis=0)

    @pl.loop(1, 16)
    def _(i):
        apcopy(i).start()
    ar_p[pl.ds(p, 1)] = ar_src[...][None]
    ring_slots(1, 14, 20)

    @pl.loop(1, 16)
    def _(i):
        apcopy(i).wait()
    sums = jnp.sum(ar_p[...], axis=0)
    sum_exp = sums[0:1, :]
    loss_out[...] = jnp.log(sum_exp) - sums[1:2, :]

    @pl.loop(0, 5)
    def _(i):
        r = pl.ds(pl.multiple_of(i * 128, 128), 128)
        t = tanh_buf[r, :]
        hit = (row_ids(i, 128) == tgt).astype(F32)
        d = (jnp.exp(30.0 * t) / sum_exp - hit) * (1.0 - t * t)
        dlt[r, :] = d.astype(BF)
        dl[:, r] = d.T.astype(BF)

    ring_slots(1, 20, SLOTS)

    def products(half):
        @pl.loop(0, 3)
        def _(i):
            n = pl.ds(pl.multiple_of(half * HALF + i * 768, 128), 768)
            g = jnp.dot(dl[...], w[:, n], preferred_element_type=F32)
            g_buf[:, :, :, n] = g.astype(BF).reshape(2, 8, 32, 768)

    def pcopy(j):
        z = lax.rem(zz + j, 8)
        return rcopy(g_buf.at[:, z, :, mate_cols], pair.at[:, z], ps.at[j], pr.at[j], p, mate)

    order = (4, 3, 5, 2, 6, 1, 7, 0)
    products(1 - core)
    for j in order:
        pcopy(j).start()
    products(core)

    def paired(y, z, c):
        return g_buf[y, z, :, pl.ds(c * HALF, HALF)].astype(F32) + pair[y, z].astype(F32)

    def rdest(d, s):
        return lax.rem(zz + 4 - s, 8) if d == 0 else lax.rem(zz + 4 + s, 8)

    def jdest(d, s):
        return 4 - s if d == 0 else lax.rem(4 + s, 8)

    def rpart(ref, c, *at):
        return ref.at[(*at, pl.ds(0, 16), pl.ds(0, QUART))] if c == 0 else ref.at[at]

    def rsend(c, d, s, y):
        z = rdest(d, s)
        src = piece(pair, y, z, xx) if c == 0 else pair.at[y, z]
        return rcopy(src, rpart(rbuf, c, d, s, y), rs.at[d, s, y], rr.at[d, s, y], zup if d == 0 else zdn, v)

    def rhas(d, s, y):
        return s > 0 or y == d

    def rstep(c, d, s, total_of):
        for y in range(2):
            if rhas(d, s, y):
                z = rdest(d, s)
                total = total_of(y, jdest(d, s))
                if s > 0 and rhas(d, s - 1, y):
                    rsend(c, d, s - 1, y).wait_recv()
                    total += rpart(rbuf, c, d, s - 1, y)[...].astype(F32)
                (piece(pair, y, z, xx) if c == 0 else pair.at[y, z])[...] = total.astype(BF)
                rsend(c, d, s, y).start()

    def zof(j):
        return lax.rem(zz + j, 8)

    def x1copy(y, j):
        z = zof(j)
        return rcopy(piece(pair, y, z, x_at(2)), xr1.at[y, z], x1s.at[y, z], x1r.at[y, z], p, x_dev(1 if y == 0 else 3))

    def x2copy(d, y, j):
        z = zof(j)
        to = 1 if d == 0 else 3
        return rcopy(piece(pair, y, z, x_at(to)), xr2.at[d, y, z], x2s.at[d, y, z], x2r.at[d, y, z], p, x_dev(to))

    def xtotal(y, j):
        z = zof(j)
        return piece(pair, y, z, xx)[...].astype(F32) + xr2[0, y, z].astype(F32) + xr2[1, y, z].astype(F32)

    blocks = [(y, j) for j in order for y in range(2)]
    zsteps = {4: [(0, 0), (1, 0)], 3: [(0, 1)], 5: [(1, 1)], 2: [(0, 2)], 6: [(1, 2)], 1: [(0, 3)], 7: [(1, 3)], 0: []}

    def reduce0(i):
        if i < 16:
            y, j = blocks[i]
            if y == 0:
                pcopy(j).wait_recv()
            pair[y, zof(j)] = paired(y, zof(j), 0).astype(BF)
            x1copy(y, j).start()
        if RLAG <= i < 16 + RLAG:
            y, j = blocks[i - RLAG]
            x1copy(y, j).wait_recv()
            b = piece(pair, y, zof(j), x_at(1 if y == 0 else 3))
            b[...] = (b[...].astype(F32) + xr1[y, zof(j)].astype(F32)).astype(BF)
            for d in range(2):
                x2copy(d, y, j).start()
        if i >= 2 * RLAG:
            y, j = blocks[i - 2 * RLAG]
            for d in range(2):
                x2copy(d, y, j).wait_recv()
            if y == 1:
                for d, s in zsteps[j]:
                    rstep(0, d, s, xtotal)

    def reduce1(i):
        j = order[i]
        pcopy(j).wait_recv()
        for d, s in zsteps[j]:
            rstep(1, d, s, lambda y, j: paired(y, zof(j), 1))

    def gcopy(i):
        return pltpu.make_async_copy(g_stage.at[i % 2], grad_out.at[:, i * 512 : (i + 1) * 512], gs.at[i % 2])

    def table(i):
        n = slice(i * 512, (i + 1) * 512)
        sel = (
            base + lax.broadcasted_iota(jnp.int32, (ROWS, TOKENS), 0) == ids_ref[...]
        ).astype(F32).astype(BF)
        acc = jnp.dot(sel, c_buf[:, :, :, n].reshape(TOKENS, 512), preferred_element_type=F32) * (float(D) ** 0.5)
        acc += jnp.dot(dlt[...], h_buf[:, :, :, n].reshape(TOKENS, 512), preferred_element_type=F32)
        if i >= 2:
            gcopy(i - 2).wait()
        g_stage[i % 2] = acc.astype(BF)
        gcopy(i).start()

    ring_finish(1)
    for i in range(16 + 2 * RLAG):
        @on_core(0)
        def _():
            reduce0(i)

        if i % 2 == 0 and i < 16:
            @on_core(1)
            def _():
                reduce1(i // 2)

        if i % 2 == 0 and i < 18:
            table(i // 2)

    def last(c, y):
        total = xtotal(y, 0) if c == 0 else paired(y, zz, 1)
        for d in range(2):
            total += rpart(rbuf, c, d, 3, y)[...].astype(F32)
        return total

    def yback(c):
        return rcopy(rpart(y_buf, c, 0), rpart(y_buf, c, 1), yys, yyr, other_y, v)

    def owner(c, k):
        return xx // 2 * 4 + k if c == 0 else 8 + k

    def vcopy(c, k):
        slot = ylo * 2 + lax.rem(xx, 2) if c == 0 else v // 2
        if c == 0:
            return rcopy(v_src.at[k, pl.ds(0, 16)], v_buf.at[slot, pl.ds(0, 16)], vs.at[k], vr.at[slot], p, owner(c, k))
        return rcopy(v_src.at[k], v_buf.at[slot], vs.at[k], vr.at[slot], p, owner(c, k))

    for c in range(2):
        @on_core(c)
        def _():
            for d in range(2):
                for y in range(2):
                    rsend(c, d, 3, y).wait_recv()
            rpart(y_buf, c, 0)[...] = last(c, 1 - yh).astype(BF)
            yback(c).start()
            mine = last(c, yh)
            yback(c).wait()
            mine += rpart(y_buf, c, 1)[...].astype(F32)
            rows = 16 if c == 0 else 32
            count = 4 if c == 0 else 8
            for k in range(count):
                v_src[k, 0:rows] = mine[:, k * PIECE : (k + 1) * PIECE]
            for k in range(count):
                @pl.when(owner(c, k) != v)
                def _():
                    vcopy(c, k).start()

                @pl.when(owner(c, k) == v)
                def _():
                    slot = ylo * 2 + lax.rem(xx, 2) if c == 0 else v // 2
                    v_buf[pl.ds(slot, 1), 0:rows] = v_src[k, 0:rows][None]

    @pl.when(v < 8)
    def _():
        for j in range(4):
            @pl.when((j // 2) * 8 + (v // 4 * 2 + j % 2) * 2 != v)
            def _():
                b = v_buf.at[j, pl.ds(0, 16)]
                rcopy(v_src.at[0, pl.ds(0, 16)], b, vs.at[0], vr.at[j], p, mate).wait_recv()
        for r in range(2):
            hid_out[16 * r : 16 * r + 16, :] = v_buf[r, 0:16] + v_buf[2 + r, 0:16]

    @pl.when(v >= 8)
    def _():
        for j in range(8):
            @pl.when(2 * j + 1 != v)
            def _():
                rcopy(v_src.at[0], v_buf.at[j], vs.at[0], vr.at[j], p, mate).wait_recv()
        hid_out[...] = jnp.sum(v_buf[...], axis=0)

    gcopy(7).wait()
    gcopy(8).wait()
    for a in range(2):
        ring_drain(a)
    for j in order:
        pcopy(j).wait_send()
    for c in range(2):
        @on_core(c)
        def _():
            for k in range(4 if c == 0 else 8):
                @pl.when(owner(c, k) != v)
                def _():
                    vcopy(c, k).wait_send()
            for s in range(4):
                for d in range(2):
                    for y in range(2):
                        if rhas(d, s, y):
                            rsend(c, d, s, y).wait_send()
            if c == 0:
                for y, j in blocks:
                    x1copy(y, j).wait_send()
                    for d in range(2):
                        x2copy(d, y, j).wait_send()


def local(final_hidden, tied_table, target_ids, input_ids, embed_cot):
    vm = pl.BlockSpec(memory_space=pltpu.VMEM)
    sem = pltpu.SemaphoreType.DMA
    grad, hid, loss = pl.pallas_call(
        kernel,
        out_shape=[
            jax.ShapeDtypeStruct((ROWS, D), BF),
            jax.ShapeDtypeStruct((32, PIECE), F32),
            jax.ShapeDtypeStruct((1, TOKENS), F32),
        ],
        in_specs=[vm, pl.BlockSpec(memory_space=pl.ANY), vm, vm, vm],
        out_specs=[pl.BlockSpec(memory_space=pl.ANY), vm, vm],
        scratch_shapes=[
            pltpu.VMEM((ROWS, D), BF),
            pltpu.VMEM((2, 8, 32, D), BF),
            pltpu.VMEM((2, 8, 32, D), BF),
            pltpu.VMEM((ROWS, TOKENS), F32),
            pltpu.VMEM((TOKENS, ROWS), BF),
            pltpu.VMEM((ROWS, TOKENS), BF),
            pltpu.VMEM((2, 8, 32, HALF), BF),
            pltpu.VMEM((2, 4, 2, 32, HALF), BF),
            pltpu.VMEM((2, 8, 32, D), BF),
            pltpu.VMEM((2, 8, 32, PIECE), BF),
            pltpu.VMEM((8, TOKENS), F32),
            pltpu.VMEM((16, 8, TOKENS), F32),
            pltpu.VMEM((16, 8, TOKENS), F32),
            pltpu.VMEM((2, 32, HALF), BF),
            pltpu.VMEM((8, 32, PIECE), F32),
            pltpu.VMEM((8, 32, PIECE), F32),
            pltpu.VMEM((2, 8, 16, QUART), BF),
            pltpu.VMEM((2, 2, 8, 16, QUART), BF),
            sem, sem((2, 8)), sem((2, 8)), sem((2,)), sem((2,)),
            sem((2, 2, 4, 2)), sem((2, 2, 4, 2)), sem((2, 2, 8)), sem((2, 2, 8)),
            sem((16,)), sem((16,)), sem((16,)), sem((16,)),
            sem((8,)), sem((8,)), sem((2, 4, 2)), sem((2, 4, 2)), sem, sem, sem((8,)), sem((8,)),
            sem((2, 2, 2, 2, 8)), sem((2, 2, 2, 2, 8)), sem((2, 8)), sem((2, 8)), sem((2, 2, 8)), sem((2, 2, 8)), sem((2,)), pltpu.VMEM((2, ROWS, 512), BF),
        ],
        compiler_params=pltpu.CompilerParams(
            collective_id=0, has_side_effects=True, vmem_limit_bytes=63 << 20
        ),
        name="head_backward",
    )(
        final_hidden,
        tied_table,
        target_ids.reshape(1, TOKENS),
        input_ids.reshape(1, TOKENS),
        embed_cot,
    )
    held = final_hidden.shape[0]
    loss_shard = lax.dynamic_slice_in_dim(loss[0], lax.axis_index("pipe") * held, held)
    return (grad, hid, loss_shard)


def solution(mesh):
    placed = (P("pipe", "vocab"), P(("pipe", "vocab"), None), P(), P(), P("pipe", "vocab"))
    return jax.shard_map(
        local,
        mesh=mesh,
        in_specs=placed,
        out_specs=(P(("pipe", "vocab"), None), P("pipe", "vocab"), P("pipe")),
        check_vma=False,
    )
```

time: 155 us -> 126 us (0.81)
  Pallas kernels: 147 us -> 118 us
    pallas_call x1, Pallas kernels: 147 us -> 118 us  [local(): pl.pallas_call(kernel, out_shape=[jax.ShapeDtypeStruct((ROWS, D), BF), ja...]
where the time goes in v2:
time: 126 us
  Pallas kernels  118 us (94%)
  local copies, waits for them, and re-layouts  7.45 us (6%)
    pallas_call x1, Pallas kernels, local(): pl.pallas_call(kernel, out_shape=[jax.ShapeDtypeStruct((ROWS, D), BF), ja...  118 us
    unnamed x4, local copies, waits for them, and re-layouts  6.25 us

profile of v2, /device:TPU:1, one launch (start us, length us, event | category | flops | bytes accessed | tf_op | source)
XLA Modules:
  0.0 126.2 jit_solution(17654965995863493834)
XLA Ops:
  0.6 118.1 %head_backward.1 = (bf16[640,4608]{1,0:T(8,128)(2,1)}, f32[32,288]{1,0:T(8,128)}, f32[1,512]{1,0:T(1,128)}) custom-call(bf16[32,288]{1,0:T(8,128)(2,1)} %h_in.1, bf16[640,4608]{1,0:T(8,128)(2,1)} %w_hbm.1, s32[1,512]{1,0:T(1,128)} %bitcast.4, s32[1,512]{1,0:T(1,128)} %bitcast.5, bf16[32,288]{1,0:T(8,128)(2,1)} %c_in.1), custom_call_target="tpu_custom_call" | custom-call | tf_op jit(solution)/shard_map/head_backward/pallas_call | solution.py:509
  118.7 1.2 dynamic-slice_bitcast_fusion
  119.9 0.0 copy-start
  119.9 5.6 %copy.10 = bf16[640,4608]{1,0:T(8,128)(2,1)} copy(bf16[640,4608]{1,0:T(8,128)(2,1)} %get-tuple-element.12) | data formatting | bytes 11796480
  125.6 0.0 copy-done
  125.6 0.6 copy.11
Async XLA Ops:
  119.9 5.6 %copy-start = (f32[32,288]{1,0:T(8,128)S(1)}, f32[32,288]{1,0:T(8,128)}, u32[]{:S(2)}) copy-start(f32[32,288]{1,0:T(8,128)} %get-tuple-element.13) | copy-start | bytes 110596

commit v3 on v2

--- a/solution.py
+++ b/solution.py
@@ -30,7 +30,7 @@
     h_in, w_hbm, tgt_ref, ids_ref, c_in,
     grad_out, hid_out, loss_out,
     w, h_buf, c_buf, tanh_buf, dl, dlt, pair, rbuf, g_buf,
-    s1, ar_src, ar_v, ar_p, y_buf, v_src, v_buf,
+    s1, sums, ar_src, ar_v, ar_p, y_buf, v_src, v_buf,
     xr1, xr2,
     w_sem, s1s, s1r, ys, yr, zs, zr, cs, cr, avs, avr, aps, apr, ps, pr, rs, rr, yys, yyr, vs, vr,
     xs, xr, x1s, x1r, x2s, x2r, gs, g_stage,
@@ -56,9 +56,10 @@
     @pl.loop(1, 16)
     def _(i):
         pl.semaphore_signal(bar, inc=1, device_id=(p, lax.rem(v + i, 16)), device_id_type=MESH)
-        pl.semaphore_signal(bar, inc=1, device_id=(lax.rem(p + i, 16), v), device_id_type=MESH)
-
-    pl.semaphore_wait(bar, 30)
+
+    for q in (other_y, zup, zdn):
+        pl.semaphore_signal(bar, inc=1, device_id=(q, v), device_id_type=MESH)
+    pl.semaphore_wait(bar, 18)
 
     bufs = (h_buf, c_buf)
     ins = (h_in, c_in)
@@ -113,18 +114,18 @@
             y, z, pl.ds(pl.multiple_of(lax.rem(x, 2) * 16, 16), 16), pl.ds(pl.multiple_of(x // 2 * QUART, 128), QUART)
         ]
 
-    def part(ref, c, y, z):
-        return piece(ref, y, z, xx) if c == 0 else ref.at[y, z, :, pl.ds(HALF, HALF)]
-
-    def ycopy(c, a):
-        b = part(bufs[a], c, yh, zz)
-        return rcopy(b, b, ys.at[a], yr.at[a], other_y, v)
-
-    def zcopy(c, a, d, s, k):
+    def part(ref, c, y, z, m):
+        return piece(ref, y, z, xx) if c == 0 else ref.at[y, z, :, pl.ds(HALF + m * QUART, QUART)]
+
+    def ycopy(c, a, m):
+        b = part(bufs[a], c, yh, zz, m)
+        return rcopy(b, b, ys.at[a, m], yr.at[a, m], other_y, v)
+
+    def zcopy(c, a, d, s, k, m):
         y = yh if k == 0 else 1 - yh
         z = lax.rem(zz - s + 8, 8) if d == 0 else lax.rem(zz + s, 8)
-        b = part(bufs[a], c, y, z)
-        return rcopy(b, b, zs.at[a, d, s, k], zr.at[a, d, s, k], zup if d == 0 else zdn, v)
+        b = part(bufs[a], c, y, z, m)
+        return rcopy(b, b, zs.at[a, d, s, k, m], zr.at[a, d, s, k, m], zup if d == 0 else zdn, v)
 
     def mcopy(c, a, y, z):
         b = bufs[a].at[y, z, :, pl.ds(c * HALF, HALF)]
@@ -153,22 +154,25 @@
         for c in range(2):
             @on_core(c)
             def _():
-                ycopy(c, a).start()
-                for d in range(2):
-                    zcopy(c, a, d, 0, 0).start()
+                for m in range(1 + c):
+                    ycopy(c, a, m).start()
+                    for d in range(2):
+                        zcopy(c, a, d, 0, 0, m).start()
                 mcopy(c, a, yh, zz).start()
 
     def take(c, a, e):
         k, y, z = where(e)
         if e is None:
-            ycopy(c, a).wait_recv()
-            for d in range(2):
-                zcopy(c, a, d, 0, 1).start()
+            for m in range(1 + c):
+                ycopy(c, a, m).wait_recv()
+                for d in range(2):
+                    zcopy(c, a, d, 0, 1, m).start()
         else:
             s, k, d = e
-            zcopy(c, a, d, s, k).wait_recv()
-            if s < 3 and has(d, s + 1, k):
-                zcopy(c, a, d, s + 1, k).start()
+            for m in range(1 + c):
+                zcopy(c, a, d, s, k, m).wait_recv()
+                if s < 3 and has(d, s + 1, k):
+                    zcopy(c, a, d, s + 1, k, m).start()
         if c == 1:
             mcopy(c, a, y, z).start()
         else:
@@ -209,7 +213,8 @@
         for c in range(2):
             @on_core(c)
             def _():
-                ycopy(c, a).wait_send()
+                for m in range(1 + c):
+                    ycopy(c, a, m).wait_send()
                 mcopy(c, a, yh, zz).wait_send()
                 for e in events:
                     k, y, z = where(e)
@@ -220,7 +225,8 @@
                         xcopy(a, k, 1, y, z).wait_send()
                     if e is not None:
                         s, k, d = e
-                        zcopy(c, a, d, s, k).wait_send()
+                        for m in range(1 + c):
+                            zcopy(c, a, d, s, k, m).wait_send()
 
         s1_drain(a)
 
@@ -240,7 +246,7 @@
     def row_ids(i, rows):
         return base + i * rows + lax.broadcasted_iota(jnp.int32, (rows, TOKENS), 0)
 
-    ar_src[...] = jnp.zeros_like(ar_src)
+    sums[...] = jnp.zeros_like(sums)
 
     for i in range(5):
         r = slice(i * 128, (i + 1) * 128)
@@ -248,9 +254,13 @@
         t = jnp.tanh(logits / 30.0)
         tanh_buf[r, :] = t
         capped = 30.0 * t
-        ar_src[0:1, :] += jnp.sum(jnp.exp(capped), axis=0, keepdims=True)
-        ar_src[1:2, :] += jnp.sum(jnp.where(row_ids(i, 128) == tgt, capped, 0.0), axis=0, keepdims=True)
-        ring_slots(1, 2 * i, 2 * i + 2)
+        sums[0:1, :] += jnp.sum(jnp.exp(capped), axis=0, keepdims=True)
+        sums[1:2, :] += jnp.sum(jnp.where(row_ids(i, 128) == tgt, capped, 0.0), axis=0, keepdims=True)
+        ring_slots(1, i, i + 1)
+
+    for k in range(4):
+        for r in range(2):
+            ar_src[4 * r + k : 4 * r + k + 1, :] = sums[r : r + 1, 128 * k : 128 * k + 128]
 
     def avcopy(i):
         return rcopy(ar_src, ar_v.at[v], avs.at[i], avr.at[i], p, lax.rem(v + i, 16))
@@ -262,7 +272,7 @@
     def _(i):
         avcopy(i).start()
     ar_v[pl.ds(v, 1)] = ar_src[...][None]
-    ring_slots(1, 10, 14)
+    ring_slots(1, 5, 9)
 
     @pl.loop(1, 16)
     def _(i):
@@ -273,14 +283,21 @@
     def _(i):
         apcopy(i).start()
     ar_p[pl.ds(p, 1)] = ar_src[...][None]
-    ring_slots(1, 14, 20)
+    ring_slots(1, 9, 13)
 
     @pl.loop(1, 16)
     def _(i):
         apcopy(i).wait()
-    sums = jnp.sum(ar_p[...], axis=0)
-    sum_exp = sums[0:1, :]
-    loss_out[...] = jnp.log(sum_exp) - sums[1:2, :]
+    whole = jnp.sum(ar_p[...], axis=0)
+    sum_exp = jnp.concatenate([whole[k : k + 1] for k in range(4)], axis=-1)
+    losses = jnp.log(whole[0:4]) - whole[4:8]
+    row = jnp.zeros((1, 128), F32)
+    for k in range(4):
+        row += jnp.where(p // 4 == k, losses[k : k + 1], 0.0)
+    held = jnp.zeros((1, 32), F32)
+    for k in range(4):
+        held += jnp.where(lax.rem(p, 4) == k, row[:, 32 * k : 32 * k + 32], 0.0)
+    loss_out[...] = held
 
     @pl.loop(0, 5)
     def _(i):
@@ -291,7 +308,7 @@
         dlt[r, :] = d.astype(BF)
         dl[:, r] = d.T.astype(BF)
 
-    ring_slots(1, 20, SLOTS)
+    ring_slots(1, 13, 15)
 
     def products(half):
         @pl.loop(0, 3)
@@ -308,11 +325,18 @@
     products(1 - core)
     for j in order:
         pcopy(j).start()
+    ring_slots(1, 15, 18)
     products(core)
+    ring_slots(1, 18, 20)
 
     def paired(y, z, c):
         return g_buf[y, z, :, pl.ds(c * HALF, HALF)].astype(F32) + pair[y, z].astype(F32)
 
+    def paired1(y, j, m):
+        z = lax.rem(zz + j, 8)
+        n = pl.ds(m * QUART, QUART)
+        return g_buf[y, z, :, pl.ds(HALF + m * QUART, QUART)].astype(F32) + pair[y, z, :, n].astype(F32)
+
     def rdest(d, s):
         return lax.rem(zz + 4 - s, 8) if d == 0 else lax.rem(zz + 4 + s, 8)
 
@@ -322,10 +346,15 @@
     def rpart(ref, c, *at):
         return ref.at[(*at, pl.ds(0, 16), pl.ds(0, QUART))] if c == 0 else ref.at[at]
 
-    def rsend(c, d, s, y):
-        z = rdest(d, s)
-        src = piece(pair, y, z, xx) if c == 0 else pair.at[y, z]
-        return rcopy(src, rpart(rbuf, c, d, s, y), rs.at[d, s, y], rr.at[d, s, y], zup if d == 0 else zdn, v)
+    def rsrc(c, y, z, m):
+        return piece(pair, y, z, xx) if c == 0 else pair.at[y, z, :, pl.ds(m * QUART, QUART)]
+
+    def rdst(c, d, s, y, m):
+        return rbuf.at[d, s, y, pl.ds(0, 32 if c else 16), pl.ds(m * QUART, QUART)]
+
+    def rsend(c, d, s, y, m):
+        src = rsrc(c, y, rdest(d, s), m)
+        return rcopy(src, rdst(c, d, s, y, m), rs.at[d, s, y, m], rr.at[d, s, y, m], zup if d == 0 else zdn, v)
 
     def rhas(d, s, y):
         return s > 0 or y == d
@@ -334,12 +363,13 @@
         for y in range(2):
             if rhas(d, s, y):
                 z = rdest(d, s)
-                total = total_of(y, jdest(d, s))
-                if s > 0 and rhas(d, s - 1, y):
-                    rsend(c, d, s - 1, y).wait_recv()
-                    total += rpart(rbuf, c, d, s - 1, y)[...].astype(F32)
-                (piece(pair, y, z, xx) if c == 0 else pair.at[y, z])[...] = total.astype(BF)
-                rsend(c, d, s, y).start()
+                for m in range(1 + c):
+                    total = total_of(y, jdest(d, s), m)
+                    if s > 0 and rhas(d, s - 1, y):
+                        rsend(c, d, s - 1, y, m).wait_recv()
+                        total += rdst(c, d, s - 1, y, m)[...].astype(F32)
+                    rsrc(c, y, z, m)[...] = total.astype(BF)
+                    rsend(c, d, s, y, m).start()
 
     def zof(j):
         return lax.rem(zz + j, 8)
@@ -353,7 +383,7 @@
         to = 1 if d == 0 else 3
         return rcopy(piece(pair, y, z, x_at(to)), xr2.at[d, y, z], x2s.at[d, y, z], x2r.at[d, y, z], p, x_dev(to))
 
-    def xtotal(y, j):
+    def xtotal(y, j, m=0):
         z = zof(j)
         return piece(pair, y, z, xx)[...].astype(F32) + xr2[0, y, z].astype(F32) + xr2[1, y, z].astype(F32)
 
@@ -386,7 +416,7 @@
         j = order[i]
         pcopy(j).wait_recv()
         for d, s in zsteps[j]:
-            rstep(1, d, s, lambda y, j: paired(y, zof(j), 1))
+            rstep(1, d, s, paired1)
 
     def gcopy(i):
         return pltpu.make_async_copy(g_stage.at[i % 2], grad_out.at[:, i * 512 : (i + 1) * 512], gs.at[i % 2])
@@ -403,7 +433,6 @@
         g_stage[i % 2] = acc.astype(BF)
         gcopy(i).start()
 
-    ring_finish(1)
     for i in range(16 + 2 * RLAG):
         @on_core(0)
         def _():
@@ -414,8 +443,12 @@
             def _():
                 reduce1(i // 2)
 
-        if i % 2 == 0 and i < 18:
-            table(i // 2)
+        if i < 5:
+            ring_slots(1, 20 + i, 21 + i)
+        elif i == 5:
+            ring_finish(1)
+        if i >= 5 and i % 2 == 1:
+            table((i - 5) // 2)
 
     def last(c, y):
         total = xtotal(y, 0) if c == 0 else paired(y, zz, 1)
@@ -440,7 +473,8 @@
         def _():
             for d in range(2):
                 for y in range(2):
-                    rsend(c, d, 3, y).wait_recv()
+                    for m in range(1 + c):
+                        rsend(c, d, 3, y, m).wait_recv()
             rpart(y_buf, c, 0)[...] = last(c, 1 - yh).astype(BF)
             yback(c).start()
             mine = last(c, yh)
@@ -495,7 +529,8 @@
                 for d in range(2):
                     for y in range(2):
                         if rhas(d, s, y):
-                            rsend(c, d, s, y).wait_send()
+                            for m in range(1 + c):
+                                rsend(c, d, s, y, m).wait_send()
             if c == 0:
                 for y, j in blocks:
                     x1copy(y, j).wait_send()
@@ -511,9 +546,9 @@
         out_shape=[
             jax.ShapeDtypeStruct((ROWS, D), BF),
             jax.ShapeDtypeStruct((32, PIECE), F32),
-            jax.ShapeDtypeStruct((1, TOKENS), F32),
+            jax.ShapeDtypeStruct((1, 32), F32),
         ],
-        in_specs=[vm, pl.BlockSpec(memory_space=pl.ANY), vm, vm, vm],
+        in_specs=[vm, pl.BlockSpec(memory_space=pltpu.HBM), vm, vm, vm],
         out_specs=[pl.BlockSpec(memory_space=pl.ANY), vm, vm],
         scratch_shapes=[
             pltpu.VMEM((ROWS, D), BF),
@@ -527,21 +562,22 @@
             pltpu.VMEM((2, 8, 32, D), BF),
             pltpu.VMEM((2, 8, 32, PIECE), BF),
             pltpu.VMEM((8, TOKENS), F32),
-            pltpu.VMEM((16, 8, TOKENS), F32),
-            pltpu.VMEM((16, 8, TOKENS), F32),
+            pltpu.VMEM((8, 128), F32),
+            pltpu.VMEM((16, 8, 128), F32),
+            pltpu.VMEM((16, 8, 128), F32),
             pltpu.VMEM((2, 32, HALF), BF),
             pltpu.VMEM((8, 32, PIECE), F32),
             pltpu.VMEM((8, 32, PIECE), F32),
             pltpu.VMEM((2, 8, 16, QUART), BF),
             pltpu.VMEM((2, 2, 8, 16, QUART), BF),
-            sem, sem((2, 8)), sem((2, 8)), sem((2,)), sem((2,)),
-            sem((2, 2, 4, 2)), sem((2, 2, 4, 2)), sem((2, 2, 8)), sem((2, 2, 8)),
+            sem, sem((2, 8)), sem((2, 8)), sem((2, 2)), sem((2, 2)),
+            sem((2, 2, 4, 2, 2)), sem((2, 2, 4, 2, 2)), sem((2, 2, 8)), sem((2, 2, 8)),
             sem((16,)), sem((16,)), sem((16,)), sem((16,)),
-            sem((8,)), sem((8,)), sem((2, 4, 2)), sem((2, 4, 2)), sem, sem, sem((8,)), sem((8,)),
+            sem((8,)), sem((8,)), sem((2, 4, 2, 2)), sem((2, 4, 2, 2)), sem, sem, sem((8,)), sem((8,)),
             sem((2, 2, 2, 2, 8)), sem((2, 2, 2, 2, 8)), sem((2, 8)), sem((2, 8)), sem((2, 2, 8)), sem((2, 2, 8)), sem((2,)), pltpu.VMEM((2, ROWS, 512), BF),
         ],
         compiler_params=pltpu.CompilerParams(
-            collective_id=0, has_side_effects=True, vmem_limit_bytes=63 << 20
+            collective_id=0, has_side_effects=True, vmem_limit_bytes=47 << 20
         ),
         name="head_backward",
     )(
@@ -551,9 +587,7 @@
         input_ids.reshape(1, TOKENS),
         embed_cot,
     )
-    held = final_hidden.shape[0]
-    loss_shard = lax.dynamic_slice_in_dim(loss[0], lax.axis_index("pipe") * held, held)
-    return (grad, hid, loss_shard)
+    return (grad, hid, loss.reshape(32))
 
 
 def solution(mesh):

time: 126 us -> 116 us (0.921)
  Pallas kernels: 118 us -> 108 us
    pallas_call x1, Pallas kernels: 118 us -> 108 us  [local(): pl.pallas_call(kernel, out_shape=[jax.ShapeDtypeStruct((ROWS, D), BF), ja...]
    unnamed x4 -> x11, local copies, waits for them, and re-layouts: 6.25 us -> 6.54 us
where the time goes in v3:
time: 116 us
  Pallas kernels  108 us (93%)
  local copies, waits for them, and re-layouts  6.54 us (6%)
    pallas_call x1, Pallas kernels, local(): pl.pallas_call(kernel, out_shape=[jax.ShapeDtypeStruct((ROWS, D), BF), ja...  108 us
    unnamed x11, local copies, waits for them, and re-layouts  6.54 us

profile of v3, /device:TPU:1, one launch (start us, length us, event | category | flops | bytes accessed | tf_op | source)
XLA Modules:
  0.0 115.5 jit_solution(4149110638121517970)
XLA Ops:
  0.6 0.0 copy-start
  0.6 0.7 copy-done
  1.4 0.0 copy-start.1
  1.4 0.7 copy-done.1
  2.1 0.0 copy-start.2
  2.1 0.7 copy-done.2
  2.8 0.0 copy-start.3
  2.8 0.7 copy-done.3
  3.5 108.3 %head_backward.1 = (bf16[640,4608]{1,0:T(8,128)(2,1)S(1)}, f32[32,288]{1,0:T(8,128)S(1)}, f32[1,32]{1,0:T(1,128)S(1)}) custom-call(bf16[32,288]{1,0:T(8,128)(2,1)S(1)} %copy-done, bf16[640,4608]{1,0:T(8,128)(2,1)} %w_hbm.1, s32[1,512]{1,0:T(1,128)S(1)} %bitcast.3, s32[1,512]{1,0:T(1,128)S(1)} %bitcast.4, bf16[32,288]{1,0:T(8,128)(2,1)S(1)} %copy-done.1), custom_call_target="tpu_custom_call" | custom-call | tf_op jit(solution)/shard_map/head_backward/pallas_call | solution.py:544
  111.8 2.6 %copy.11 = bf16[640,4608]{1,0:T(8,128)(2,1)} copy(bf16[640,4608]{1,0:T(8,128)(2,1)S(1)} %get-tuple-element.12) | data formatting | bytes 11796480
  114.4 0.6 copy.12
  115.0 0.5 copy.13
Async XLA Ops:
  0.6 0.7 copy-start
  1.4 0.7 copy-start.1
  2.1 0.7 copy-start.2
  2.8 0.7 copy-start.3

commit v4 on v3

--- a/solution.py
+++ b/solution.py
@@ -8,8 +8,9 @@
 D = 4608
 HALF = D // 2
 QUART = D // 4
-LAG = 5
-RLAG = 3
+LAG = 6
+RLAG = 4
+FIRST = 7
 SLOTS = 15 + 2 * LAG
 ROWS = 640
 TOKENS = 512
@@ -251,7 +252,7 @@
     for i in range(5):
         r = slice(i * 128, (i + 1) * 128)
         logits = lax.dot_general(w[r, :], h_buf[...].reshape(TOKENS, D), NT, preferred_element_type=F32)
-        t = jnp.tanh(logits / 30.0)
+        t = jnp.tanh(logits * (1.0 / 30.0))
         tanh_buf[r, :] = t
         capped = 30.0 * t
         sums[0:1, :] += jnp.sum(jnp.exp(capped), axis=0, keepdims=True)
@@ -290,6 +291,7 @@
         apcopy(i).wait()
     whole = jnp.sum(ar_p[...], axis=0)
     sum_exp = jnp.concatenate([whole[k : k + 1] for k in range(4)], axis=-1)
+    inverse = 1.0 / sum_exp
     losses = jnp.log(whole[0:4]) - whole[4:8]
     row = jnp.zeros((1, 128), F32)
     for k in range(4):
@@ -304,7 +306,7 @@
         r = pl.ds(pl.multiple_of(i * 128, 128), 128)
         t = tanh_buf[r, :]
         hit = (row_ids(i, 128) == tgt).astype(F32)
-        d = (jnp.exp(30.0 * t) / sum_exp - hit) * (1.0 - t * t)
+        d = (jnp.exp(30.0 * t) * inverse - hit) * (1.0 - t * t)
         dlt[r, :] = d.astype(BF)
         dl[:, r] = d.T.astype(BF)
 
@@ -443,21 +445,26 @@
             def _():
                 reduce1(i // 2)
 
-        if i < 5:
+        if i < SLOTS - 20:
             ring_slots(1, 20 + i, 21 + i)
-        elif i == 5:
+        if i == FIRST:
             ring_finish(1)
-        if i >= 5 and i % 2 == 1:
-            table((i - 5) // 2)
-
-    def last(c, y):
-        total = xtotal(y, 0) if c == 0 else paired(y, zz, 1)
+        if FIRST <= i < FIRST + 9:
+            table(i - FIRST)
+
+    def last(c, y, m):
         for d in range(2):
-            total += rpart(rbuf, c, d, 3, y)[...].astype(F32)
+            rsend(c, d, 3, y, m).wait_recv()
+        total = xtotal(y, 0) if c == 0 else paired1(y, 0, m)
+        for d in range(2):
+            total += rdst(c, d, 3, y, m)[...].astype(F32)
         return total
 
-    def yback(c):
-        return rcopy(rpart(y_buf, c, 0), rpart(y_buf, c, 1), yys, yyr, other_y, v)
+    def yref(c, i, m):
+        return y_buf.at[i, pl.ds(0, 32 if c else 16), pl.ds(m * QUART, QUART)]
+
+    def yback(c, m):
+        return rcopy(yref(c, 0, m), yref(c, 1, m), yys.at[m], yyr.at[m], other_y, v)
 
     def owner(c, k):
         return xx // 2 * 4 + k if c == 0 else 8 + k
@@ -471,28 +478,25 @@
     for c in range(2):
         @on_core(c)
         def _():
-            for d in range(2):
-                for y in range(2):
-                    for m in range(1 + c):
-                        rsend(c, d, 3, y, m).wait_recv()
-            rpart(y_buf, c, 0)[...] = last(c, 1 - yh).astype(BF)
-            yback(c).start()
-            mine = last(c, yh)
-            yback(c).wait()
-            mine += rpart(y_buf, c, 1)[...].astype(F32)
             rows = 16 if c == 0 else 32
-            count = 4 if c == 0 else 8
-            for k in range(count):
-                v_src[k, 0:rows] = mine[:, k * PIECE : (k + 1) * PIECE]
-            for k in range(count):
-                @pl.when(owner(c, k) != v)
-                def _():
-                    vcopy(c, k).start()
-
-                @pl.when(owner(c, k) == v)
-                def _():
-                    slot = ylo * 2 + lax.rem(xx, 2) if c == 0 else v // 2
-                    v_buf[pl.ds(slot, 1), 0:rows] = v_src[k, 0:rows][None]
+            for m in range(1 + c):
+                yref(c, 0, m)[...] = last(c, 1 - yh, m).astype(BF)
+                yback(c, m).start()
+            for m in range(1 + c):
+                mine = last(c, yh, m)
+                yback(c, m).wait_recv()
+                mine += yref(c, 1, m)[...].astype(F32)
+                for i in range(4):
+                    v_src[4 * m + i, 0:rows] = mine[:, i * PIECE : (i + 1) * PIECE]
+                for k in range(4 * m, 4 * m + 4):
+                    @pl.when(owner(c, k) != v)
+                    def _():
+                        vcopy(c, k).start()
+
+                    @pl.when(owner(c, k) == v)
+                    def _():
+                        slot = ylo * 2 + lax.rem(xx, 2) if c == 0 else v // 2
+                        v_buf[pl.ds(slot, 1), 0:rows] = v_src[k, 0:rows][None]
 
     @pl.when(v < 8)
     def _():
@@ -521,6 +525,8 @@
     for c in range(2):
         @on_core(c)
         def _():
+            for m in range(1 + c):
+                yback(c, m).wait_send()
             for k in range(4 if c == 0 else 8):
                 @pl.when(owner(c, k) != v)
                 def _():
@@ -573,7 +579,7 @@
             sem, sem((2, 8)), sem((2, 8)), sem((2, 2)), sem((2, 2)),
             sem((2, 2, 4, 2, 2)), sem((2, 2, 4, 2, 2)), sem((2, 2, 8)), sem((2, 2, 8)),
             sem((16,)), sem((16,)), sem((16,)), sem((16,)),
-            sem((8,)), sem((8,)), sem((2, 4, 2, 2)), sem((2, 4, 2, 2)), sem, sem, sem((8,)), sem((8,)),
+            sem((8,)), sem((8,)), sem((2, 4, 2, 2)), sem((2, 4, 2, 2)), sem((2,)), sem((2,)), sem((8,)), sem((8,)),
             sem((2, 2, 2, 2, 8)), sem((2, 2, 2, 2, 8)), sem((2, 8)), sem((2, 8)), sem((2, 2, 8)), sem((2, 2, 8)), sem((2,)), pltpu.VMEM((2, ROWS, 512), BF),
         ],
         compiler_params=pltpu.CompilerParams(

time: 116 us -> 114 us (0.983)
    pallas_call x1, Pallas kernels: 108 us -> 107 us  [local(): pl.pallas_call(kernel, out_shape=[jax.ShapeDtypeStruct((ROWS, D), BF), ja...]
where the time goes in v4:
time: 114 us
  Pallas kernels  107 us (94%)
  local copies, waits for them, and re-layouts  6.54 us (6%)
    pallas_call x1, Pallas kernels, local(): pl.pallas_call(kernel, out_shape=[jax.ShapeDtypeStruct((ROWS, D), BF), ja...  107 us
    unnamed x11, local copies, waits for them, and re-layouts  6.54 us

profile of v4, /device:TPU:1, one launch (start us, length us, event | category | flops | bytes accessed | tf_op | source)
XLA Modules:
  0.0 113.8 jit_solution(3667512648727207842)
XLA Ops:
  0.6 0.0 copy-start
  0.6 0.7 copy-done
  1.4 0.0 copy-start.1
  1.4 0.7 copy-done.1
  2.1 0.0 copy-start.2
  2.1 0.7 copy-done.2
  2.8 0.0 copy-start.3
  2.8 0.7 copy-done.3
  3.5 106.6 %head_backward.1 = (bf16[640,4608]{1,0:T(8,128)(2,1)S(1)}, f32[32,288]{1,0:T(8,128)S(1)}, f32[1,32]{1,0:T(1,128)S(1)}) custom-call(bf16[32,288]{1,0:T(8,128)(2,1)S(1)} %copy-done, bf16[640,4608]{1,0:T(8,128)(2,1)} %w_hbm.1, s32[1,512]{1,0:T(1,128)S(1)} %bitcast.3, s32[1,512]{1,0:T(1,128)S(1)} %bitcast.4, bf16[32,288]{1,0:T(8,128)(2,1)S(1)} %copy-done.1), custom_call_target="tpu_custom_call" | custom-call | tf_op jit(solution)/shard_map/head_backward/pallas_call | solution.py:550
  110.1 2.6 %copy.11 = bf16[640,4608]{1,0:T(8,128)(2,1)} copy(bf16[640,4608]{1,0:T(8,128)(2,1)S(1)} %get-tuple-element.12) | data formatting | bytes 11796480
  112.7 0.6 copy.12
  113.3 0.5 copy.13
Async XLA Ops:
  0.6 0.7 copy-start
  1.4 0.7 copy-start.1
  2.1 0.7 copy-start.2
  2.8 0.7 copy-start.3
